TPU v7x, 32 devices: a whole 2x2x4 slice. The times are simulated.
32 devices in a mesh: dp: 8 (over y, x, core), replica: 4 (over z).
Axes of the slice: x: 2, y: 2, z: 4, core: 2. Of those that a mesh axis runs over, the one named last changes fastest.
Arguments:
- gradient: bfloat16 [4, 8, 8, 8192], P('replica', 'dp'), may hold values from -6 to 6
- master: float32 [8, 8192], P('dp', 'replica'), may hold values from -0.0625 to 0.0625
- moment: float32 [8, 8192], P('dp', 'replica'), may hold values from -0.046875 to 0.046875
- second: float32 [8, 8192], P('dp', 'replica'), may hold values from 1e-06 to 0.0001
Outputs:
- new_params: bfloat16 [8, 8192], P('dp')
- new_master: float32 [8, 8192], P('dp', 'replica')
- new_moment: float32 [8, 8192], P('dp', 'replica')
- new_second: float32 [8, 8192], P('dp', 'replica')
- direction: float32 [8, 8192], P('dp', 'replica')
- ratios: float32 [4], replicated
All inputs are finite; a program needn't handle non-finite values.
Results may differ from a plain program's by a relative error of at most 0.001.
Values may be sent and summed in bfloat16 or wider, within the bound.
A program may use at most 64 MiB of HBM per device.

v0:
```python
import jax
import jax.numpy as jnp
from jax import lax
from jax.sharding import PartitionSpec as P

MATS = 4
STEP = 2


def local(gradient, master, moment, second):
    raw_rows = gradient[0, 0]
    rows_all, width = raw_rows.shape
    data_count = lax.axis_size("dp")
    rep_count = lax.axis_size("replica")
    row_dev = rows_all // data_count
    terms = raw_rows.astype(jnp.float32)
    owned_rows = lax.psum_scatter(terms, "dp", scatter_dimension=0, tiled=True)
    summed = lax.psum_scatter(owned_rows, "replica", scatter_dimension=1, tiled=True)
    grad = summed / (data_count * rep_count)
    new_moment = 0.9 * moment + 0.1 * grad
    new_second = 0.999 * second + 0.001 * grad * grad
    first_fix = 1.0 - 0.9**STEP
    second_fix = 1.0 - 0.999**STEP
    direction = new_moment / first_fix / (jnp.sqrt(new_second / second_fix) + 1e-08)
    new_master = master - 0.0003 * (direction + 0.1 * master)
    row_ids = lax.axis_index("dp") * row_dev + lax.iota(jnp.int32, row_dev)
    owner_mat = row_ids // (rows_all // MATS)
    member = (owner_mat[:, None] == lax.iota(jnp.int32, MATS)[None, :]).astype(jnp.float32)
    dir_rows = jnp.sum(direction * direction, axis=1)
    wgt_rows = jnp.sum(master * master, axis=1)
    dir_part = jnp.sum(member * dir_rows[:, None], axis=0)
    wgt_part = jnp.sum(member * wgt_rows[:, None], axis=0)
    dir_sq, wgt_sq = lax.psum((dir_part, wgt_part), ("dp", "replica"))
    ratios = jnp.sqrt(dir_sq) / (jnp.sqrt(wgt_sq) + 1e-06)
    new_params = lax.all_gather(new_master.astype(jnp.bfloat16), "replica", axis=1, tiled=True)
    return (new_params, new_master, new_moment, new_second, direction, ratios)


def solution(mesh):
    return jax.shard_map(
        local,
        mesh=mesh,
        in_specs=(
            P("replica", "dp", None, None),
            P("dp", "replica"),
            P("dp", "replica"),
            P("dp", "replica"),
        ),
        out_specs=(
            P("dp", None),
            P("dp", "replica"),
            P("dp", "replica"),
            P("dp", "replica"),
            P("dp", "replica"),
            P(),
        ),
        check_vma=False,
    )
```

profile of v0, /device:TPU:0, one launch (start us, length us, event | category | flops | bytes accessed | tf_op | source)
XLA Modules:
  0.0 214.0 jit_solution(4225715408327386011)
XLA Ops:
  7.2 0.0 all-reduce.4.cloned.1.call-start
  7.2 1.6 bitcast_convert_fusion
  8.8 0.0 all-reduce.4.cloned.1.call-update
  8.9 0.0 reduce-scatter.4.cloned.1.call-start
  8.9 1.2 dynamic-slice
  10.2 57.2 %all-reduce.4.cloned.1.call-done = f32[8,8192]{1,0:T(8,128)} async-done(((f32[8,8192]{1,0:T(8,128)}), f32[8,8192]{1,0:T(8,128)}) %all-reduce.4.cloned.1.call-update) | async-done | bytes 262160
  67.3 1.6 constant_dynamic-slice_fusion
  68.9 0.0 copy-start.1
  69.0 0.0 copy-start.2
  69.0 0.0 copy-start.3
  69.0 2.6 %copy.10 = f32[1,8192]{0,1:T(8,128)} copy(f32[1,8192]{1,0:T(1,128)S(1)} %constant_dynamic-slice_fusion) | data formatting | bytes 65536
  71.6 0.0 reduce-scatter.4.cloned.1.call-update
  71.6 76.3 %reduce-scatter.4.cloned.1.call-done = f32[2048,1]{1,0:T(8,128)} async-done(((f32[8192,1]{1,0:T(8,128)}), f32[2048,1]{1,0:T(8,128)}) %reduce-scatter.4.cloned.1.call-update) | async-done | bytes 8208
  147.9 1.6 copy.11
  149.5 0.0 copy-done.1
  149.5 0.0 copy-done.2
  149.5 1.3 multiply_reduce_fusion.1
  150.7 0.0 copy-start
  150.7 0.0 copy-done.3
  150.7 1.2 fusion
  152.0 13.7 %all_gather.3 = bf16[1,8192]{1,0:T(2,128)(2,1)S(1)} all-gather(bf16[1,2048]{1,0:T(2,128)(2,1)S(1)} %get-tuple-element.12), channel_id=1, replica_groups=mesh['dp'=8,'replica'=4] {'replica'}, dimensions={1}, use_global_device_ids=true | all-gather | bytes 20480 | tf_op jit(solution)/shard_map/all_gather | solution.py:35
  165.6 1.3 compare_select_fusion
  166.9 39.1 %all-reduce.1 = (f32[4]{0:T(128)S(1)}, f32[4]{0:T(128)S(1)}) all-reduce(f32[4]{0:T(128)S(1)} %get-tuple-element.15, f32[4]{0:T(128)S(1)} %get-tuple-element.16), channel_id=1, replica_groups=mesh['dp'=8,'replica'=4] {'dp','replica'}, use_global_device_ids=true, to_apply=%region_5.6 | all-reduce | flops 8 | bytes 64 | tf_op jit(solution)/shard_map/psum | solution.py:33
  206.0 0.5 add_divide_fusion.1
  206.6 0.6 copy.14
  207.2 0.0 copy-done
Async XLA Ops:
  7.2 60.1 %all-reduce.4.cloned.1.call-start = ((), (), s32[]{:S(2)}) async-start(), calls=%async_computation.2 | async-start | bytes 524288
  8.9 139.1 %reduce-scatter.4.cloned.1.call-start = ((), (), s32[]{:S(2)}) async-start(), calls=%async_computation.1 | async-start | bytes 5242880
  68.9 80.5 %copy-start.1 = (f32[1,2048]{1,0:T(1,128)S(1)}, f32[1,2048]{1,0:T(1,128)}, u32[]{:S(2)}) copy-start(f32[1,2048]{1,0:T(1,128)} %param.6) | copy-start | bytes 24580
  69.0 80.5 %copy-start.2 = (f32[1,2048]{1,0:T(1,128)S(1)}, f32[1,2048]{1,0:T(1,128)}, u32[]{:S(2)}) copy-start(f32[1,2048]{1,0:T(1,128)} %param.7) | copy-start | bytes 24580
  69.0 81.8 %copy-start.3 = (f32[1,2048]{1,0:T(1,128)S(1)}, f32[1,2048]{1,0:T(1,128)}, u32[]{:S(2)}) copy-start(f32[1,2048]{1,0:T(1,128)} %param.5) | copy-start | bytes 24580
  150.7 56.4 %copy-start = (f32[1,2048]{1,0:T(1,128)}, f32[1,2048]{1,0:T(1,128)S(1)}, u32[]{:S(2)}) copy-start(f32[1,2048]{1,0:T(1,128)S(1)} %get-tuple-element.27) | copy-start | bytes 24580
Sparse Core Ops, SparseCore 0:
  11.1 56.2 all-reduce.3
  71.7 76.1 reduce-scatter.3
where the time goes:
time: 214 us
  waiting for transfers between devices  133 us (62%)
  blocking collectives  52.8 us (25%)
  between operations  14.1 us (7%)
  local copies, waits for them, and re-layouts  7.67 us (4%)
  other arithmetic  5.92 us (3%)
    unnamed x4, waiting for transfers between devices  133 us
    psum x1, blocking collectives, local(): dir_sq, wgt_sq = lax.psum((dir_part, wgt_part), ('dp', 'replica'))  39.1 us
    all_gather x1, blocking collectives, local(): lax.all_gather(new_master.astype(jnp.bfloat16), 'replica', axis=1, tiled=...  13.7 us
    unnamed x13, local copies, waits for them, and re-layouts  7.67 us
  transfers between devices with their start and end apart: 2, of which 2 were waited for; matrix products, arithmetic and copies ran while one was open for 1% of the time, Pallas kernels for 0%

commit v1 on v0

--- a/solution.py
+++ b/solution.py
@@ -30,7 +30,7 @@
     wgt_rows = jnp.sum(master * master, axis=1)
     dir_part = jnp.sum(member * dir_rows[:, None], axis=0)
     wgt_part = jnp.sum(member * wgt_rows[:, None], axis=0)
-    dir_sq, wgt_sq = lax.psum((dir_part, wgt_part), ("dp", "replica"))
+    dir_sq, wgt_sq = lax.psum(lax.psum((dir_part, wgt_part), "replica"), "dp")
     ratios = jnp.sqrt(dir_sq) / (jnp.sqrt(wgt_sq) + 1e-06)
     new_params = lax.all_gather(new_master.astype(jnp.bfloat16), "replica", axis=1, tiled=True)
     return (new_params, new_master, new_moment, new_second, direction, ratios)

time: 214 us -> 197 us (0.921)
  blocking collectives: 52.8 us -> 35.8 us
    psum x1 -> x2, blocking collectives: 39.1 us -> 22.1 us  [local(): dir_sq, wgt_sq = lax.psum(lax.psum((dir_part, wgt_part), 'replica'), 'dp')]
where the time goes in v1:
time: 197 us
  waiting for transfers between devices  133 us (68%)
  blocking collectives  35.8 us (18%)
  between operations  14.1 us (7%)
  local copies, waits for them, and re-layouts  7.67 us (4%)
  other arithmetic  5.92 us (3%)
    unnamed x4, waiting for transfers between devices  133 us
    psum x2, blocking collectives, local(): dir_sq, wgt_sq = lax.psum(lax.psum((dir_part, wgt_part), 'replica'), 'dp')  22.1 us
    all_gather x1, blocking collectives, local(): lax.all_gather(new_master.astype(jnp.bfloat16), 'replica', axis=1, tiled=...  13.7 us
    unnamed x13, local copies, waits for them, and re-layouts  7.67 us
  transfers between devices with their start and end apart: 2, of which 2 were waited for; matrix products, arithmetic and copies ran while one was open for 1% of the time, Pallas kernels for 0%

profile of v1, /device:TPU:0, one launch (start us, length us, event | category | flops | bytes accessed | tf_op | source)
XLA Modules:
  0.0 197.1 jit_solution(16382237676482239432)
XLA Ops:
  7.2 0.0 all-reduce.5.cloned.1.call-start
  7.2 1.6 bitcast_convert_fusion
  8.8 0.0 all-reduce.5.cloned.1.call-update
  8.9 0.0 reduce-scatter.4.cloned.1.call-start
  8.9 1.2 dynamic-slice
  10.2 57.2 %all-reduce.5.cloned.1.call-done = f32[8,8192]{1,0:T(8,128)} async-done(((f32[8,8192]{1,0:T(8,128)}), f32[8,8192]{1,0:T(8,128)}) %all-reduce.5.cloned.1.call-update) | async-done | bytes 262160
  67.3 1.6 constant_dynamic-slice_fusion
  68.9 0.0 copy-start.1
  69.0 0.0 copy-start.2
  69.0 0.0 copy-start.3
  69.0 2.6 %copy.10 = f32[1,8192]{0,1:T(8,128)} copy(f32[1,8192]{1,0:T(1,128)S(1)} %constant_dynamic-slice_fusion) | data formatting | bytes 65536
  71.6 0.0 reduce-scatter.4.cloned.1.call-update
  71.6 76.3 %reduce-scatter.4.cloned.1.call-done = f32[2048,1]{1,0:T(8,128)} async-done(((f32[8192,1]{1,0:T(8,128)}), f32[2048,1]{1,0:T(8,128)}) %reduce-scatter.4.cloned.1.call-update) | async-done | bytes 8208
  147.9 1.6 copy.11
  149.5 0.0 copy-done.1
  149.5 0.0 copy-done.2
  149.5 1.3 multiply_reduce_fusion.1
  150.7 0.0 copy-start
  150.7 0.0 copy-done.3
  150.7 1.2 fusion
  152.0 13.7 %all_gather.3 = bf16[1,8192]{1,0:T(2,128)(2,1)S(1)} all-gather(bf16[1,2048]{1,0:T(2,128)(2,1)S(1)} %get-tuple-element.14), channel_id=1, replica_groups=mesh['dp'=8,'replica'=4] {'replica'}, dimensions={1}, use_global_device_ids=true | all-gather | bytes 20480 | tf_op jit(solution)/shard_map/all_gather | solution.py:35
  165.6 1.3 compare_select_fusion
  166.9 10.4 %all-reduce.2 = (f32[4]{0:T(128)S(1)}, f32[4]{0:T(128)S(1)}) all-reduce(f32[4]{0:T(128)S(1)} %get-tuple-element.17, f32[4]{0:T(128)S(1)} %get-tuple-element.18), channel_id=1, replica_groups=mesh['dp'=8,'replica'=4] {'replica'}, use_global_device_ids=true, to_apply=%region_6.7 | all-reduce | flops 8 | bytes 64 | tf_op jit(solution)/shard_map/psum | solution.py:33
  177.3 11.8 %all-reduce.1 = (f32[4]{0:T(128)S(1)}, f32[4]{0:T(128)S(1)}) all-reduce(f32[4]{0:T(128)S(1)} %get-tuple-element.8, f32[4]{0:T(128)S(1)} %get-tuple-element.9), channel_id=1, replica_groups=mesh['dp'=8,'replica'=4] {'dp'}, use_global_device_ids=true, to_apply=%region_7.8 | all-reduce | flops 8 | bytes 64 | tf_op jit(solution)/shard_map/psum | solution.py:33
  189.1 0.5 add_divide_fusion.1
  189.6 0.6 copy.14
  190.2 0.0 copy-done
Async XLA Ops:
  7.2 60.1 %all-reduce.5.cloned.1.call-start = ((), (), s32[]{:S(2)}) async-start(), calls=%async_computation.2 | async-start | bytes 524288
  8.9 139.1 %reduce-scatter.4.cloned.1.call-start = ((), (), s32[]{:S(2)}) async-start(), calls=%async_computation.1 | async-start | bytes 5242880
  68.9 80.5 %copy-start.1 = (f32[1,2048]{1,0:T(1,128)S(1)}, f32[1,2048]{1,0:T(1,128)}, u32[]{:S(2)}) copy-start(f32[1,2048]{1,0:T(1,128)} %param.6) | copy-start | bytes 24580
  69.0 80.5 %copy-start.2 = (f32[1,2048]{1,0:T(1,128)S(1)}, f32[1,2048]{1,0:T(1,128)}, u32[]{:S(2)}) copy-start(f32[1,2048]{1,0:T(1,128)} %param.7) | copy-start | bytes 24580
  69.0 81.8 %copy-start.3 = (f32[1,2048]{1,0:T(1,128)S(1)}, f32[1,2048]{1,0:T(1,128)}, u32[]{:S(2)}) copy-start(f32[1,2048]{1,0:T(1,128)} %param.5) | copy-start | bytes 24580
  150.7 39.5 %copy-start = (f32[1,2048]{1,0:T(1,128)}, f32[1,2048]{1,0:T(1,128)S(1)}, u32[]{:S(2)}) copy-start(f32[1,2048]{1,0:T(1,128)S(1)} %get-tuple-element.29) | copy-start | bytes 24580
Sparse Core Ops, SparseCore 0:
  11.1 56.2 all-reduce.4
  71.7 76.1 reduce-scatter.3
